TPU v7x, 32 devices: a whole 2x2x4 slice. The times are simulated.
32 devices in a mesh: les: 8 (over y, x, core), modes: 4 (over z).
Axes of the slice: x: 2, y: 2, z: 4, core: 2. Of those that a mesh axis runs over, the one named last changes fastest.
Arguments:
- pressure: bfloat16 [65536, 512], P('les', 'modes'), may hold values from -6 to 6
- targets: int32 [65536], P('les'), may hold values from 0 to 32767, as said below
- counts: int32 [8], P('les'), may hold values from 1 to 8192, as said below
- pseudo_inverse: bfloat16 [2, 1536, 16384], P(None, None, ('les', 'modes')), may hold values from -0.046875 to 0.046875
Outputs:
- harmonics: float32 [2, 2, 8, 1536], P(None, None, None, ('les', 'modes'))
Inputs may be any that keep to these rules, and one draw needn't show every extreme that they name: `counts`: some partition holds exactly 8192 live faces; all partitions together hold 32768. `targets`: the live slots (slot f of partition i with f < counts[i]) name every station point exactly once. Point p of a station lies in the point rows of les index p // (512 * 4); at most 1024 live faces of one partition lie in the point rows of one les index, and some partition reaches that bound. Slots that are not live hold arbitrary indices in the range.
All inputs are finite; a program needn't handle non-finite values.
Results may differ from a plain program's by a relative error of at most 0.0003.
Values may be sent and summed in bfloat16 or wider, within the bound.
A program may use at most 64 MiB of HBM per device.

v0:
```python
import math
import jax
import jax.numpy as jnp
from jax import lax
from jax.sharding import PartitionSpec as P

TIME = 512
HARM = 8


def fourier_rows():
    sample_ids = jnp.arange(TIME, dtype=jnp.int32)
    orders = jnp.arange(1, HARM + 1, dtype=jnp.int32)
    phase_ids = orders[:, None] * sample_ids[None, :] % TIME
    angles = phase_ids.astype(jnp.float32) * (2.0 * math.pi / TIME)
    scale_factor = math.sqrt(2.0 / TIME)
    return jnp.stack([jnp.cos(angles), -jnp.sin(angles)]) * scale_factor


def rank_by_owner(dest_les, is_live, les_count):
    face_slots = dest_les.shape[0]
    span_width = math.gcd(face_slots, 128)
    owner_ids = jnp.arange(les_count, dtype=jnp.int32)
    matches = ((dest_les[None, :] == owner_ids[:, None]) & is_live[None, :]).astype(jnp.float32)
    matches = matches.reshape(les_count, face_slots // span_width, span_width)
    position = jnp.arange(span_width, dtype=jnp.int32)
    upper = (position[:, None] <= position[None, :]).astype(jnp.float32)
    within = jnp.einsum("nbj,jw->nbw", matches, upper, precision=lax.Precision.HIGHEST)
    block_sums = jnp.sum(matches, axis=2)
    before = jnp.cumsum(block_sums, axis=1) - block_sums
    running = within + before[:, :, None]
    ranked = jnp.sum(running * matches, axis=0).reshape(face_slots) - 1.0
    return ranked.astype(jnp.int32)


def local(pressure, targets, counts, pseudo_inverse):
    les_count = lax.axis_size("les")
    mode_count = lax.axis_size("modes")
    block_len = pressure.shape[1]
    face_slots = targets.shape[0]
    stations = pseudo_inverse.shape[0]
    mode_total = pseudo_inverse.shape[1]
    point_dev = pseudo_inverse.shape[2]
    rows_les = point_dev * mode_count
    points_all = rows_les * les_count
    send_cap = face_slots // les_count
    send_total = les_count * send_cap
    slot_ids = jnp.arange(face_slots, dtype=jnp.int32)
    is_live = slot_ids < counts[0]
    station_of = targets // points_all
    point_of = targets % points_all
    dest_les = point_of // rows_les
    local_row = station_of * rows_les + point_of % rows_les
    face_rank = rank_by_owner(dest_les, is_live, les_count)
    send_pos = jnp.where(is_live, dest_les * send_cap + face_rank, send_total)
    source_face = jnp.full((send_total,), -1, jnp.int32).at[send_pos].set(slot_ids, mode="drop")
    slot_used = source_face >= 0
    source_safe = jnp.maximum(source_face, 0)
    row_tags = jnp.where(slot_used, jnp.take(local_row, source_safe, axis=0), -1).reshape(
        1, send_total
    )
    tags_in = lax.all_to_all(row_tags, "les", split_axis=1, concat_axis=1, tiled=True)
    arrival = jnp.where(tags_in[0] >= 0, tags_in[0], stations * rows_les)
    arrival_ids = jnp.arange(send_total, dtype=jnp.int32)
    arrived_from = (
        jnp.zeros((stations * rows_les,), jnp.int32).at[arrival].set(arrival_ids, mode="drop")
    )
    fourier = fourier_rows()
    block_start = lax.axis_index("modes") * block_len
    block_rows = lax.dynamic_slice_in_dim(fourier, block_start, block_len, 2)
    block_rows = block_rows.reshape(2 * HARM, block_len)
    spectra = lax.dot_general(
        pressure.astype(jnp.float32),
        block_rows,
        (((1,), (1,)), ((), ())),
        precision=lax.Precision.HIGHEST,
    )
    picked = jnp.take(spectra, source_safe, axis=0)
    outgoing = jnp.where(slot_used[:, None], picked, jnp.zeros_like(picked))
    incoming = lax.all_to_all(outgoing, "les", split_axis=0, concat_axis=0, tiled=True)
    gathered = jnp.take(incoming, arrived_from, axis=0)
    gathered = gathered.reshape(stations, rows_les, 2 * HARM)
    summed = lax.psum_scatter(gathered, "modes", scatter_dimension=1, tiled=True)
    partial_value = []
    for station_index in range(stations):
        weights = pseudo_inverse[station_index].astype(jnp.float32)
        projected = lax.dot_general(
            summed[station_index],
            weights,
            (((0,), (1,)), ((), ())),
            precision=lax.Precision.HIGHEST,
        )
        partial_value.append(projected.reshape(2, HARM, mode_total))
    shares = jnp.stack(partial_value)
    return lax.psum_scatter(shares, ("les", "modes"), scatter_dimension=3, tiled=True)


def solution(mesh):
    placed = (P("les", "modes"), P("les"), P("les"), P(None, None, ("les", "modes")))
    return jax.shard_map(
        local,
        mesh=mesh,
        in_specs=placed,
        out_specs=P(None, None, None, ("les", "modes")),
        check_vma=False,
    )
```

profile of v0, /device:TPU:0, one launch (start us, length us, event | category | flops | bytes accessed | tf_op | source)
XLA Modules:
  0.0 323.5 jit_solution(5124301517689672651)
XLA Ops:
  7.4 0.8 fusion.13
  8.2 0.1 convert_reduce_fusion
  8.3 0.2 reduce_window_sum.11
  8.6 0.2 fusion.5
  8.8 0.8 compare_select_fusion.2
  9.6 30.5 %scatter_custom_fusion = s32[8192]{0:T(1024)S(1)} fusion(s32[8192]{0:T(1024)S(1)} %compare_select_fusion.2, s32[8192]{0:T(1024)S(1)} %iota.64, s32[]{:T(128)} %constant.117.clone.1), kind=kCustom, calls=%fused_computation.68 | custom fusion | bytes 32772 | tf_op jit(solution)/shard_map/scatter | solution.py:56
  40.1 45.5 %gather_fusion = s32[8192]{0:T(1024)S(1)} fusion(s32[8192]{0:T(1024)S(1)} %get-tuple-element.8, s32[8192]{0:T(1024)S(1)} %maximum_clamp_fusion), kind=kCustom, calls=%fused_computation | custom fusion | bytes 98304 | tf_op jit(solution)/shard_map/jit(_take)/gather | solution.py:59
  85.6 0.6 select_select_fusion.1
  86.3 5.2 %all-to-all-start = ((s32[1,8,1024]{2,0,1:T(1,128)}), s32[1,8,1024]{2,0,1:T(1,128)S(1)}, u32[]{:S(2)}, u32[]{:S(2)}) async-start(s32[1,8,1024]{2,0,1:T(1,128)} %bitcast.4), calls=%async_computation | async-start | bytes 65536 | tf_op jit(solution)/shard_map/all_to_all | solution.py:62
  91.4 0.2 sine_negate_fusion
  91.7 1.7 convolution_bitcast_fusion
  93.4 2.6 copy.9
  96.0 29.9 %gather_fusion.1 = f32[8192,16]{1,0:T(8,128)} fusion(f32[8192,16]{1,0:T(8,128)} %copy.9, s32[8192]{0:T(1024)S(1)} %maximum_clamp_fusion), kind=kCustom, calls=%fused_computation.1 | custom fusion | bytes 1081344 | tf_op jit(solution)/shard_map/jit(_take)/gather | solution.py:78
  125.9 2.8 copy.10
  128.7 0.9 select_select_fusion
  129.6 4.2 %all-to-all-start.1 = ((f32[8,1024,16]{1,2,0:T(8,128)}), f32[8,1024,16]{1,2,0:T(8,128)S(1)}, u32[]{:S(2)}, u32[]{:S(2)}) async-start(f32[8,1024,16]{1,2,0:T(8,128)} %select_select_fusion), calls=%async_computation.1 | async-start | bytes 1048576 | tf_op jit(solution)/shard_map/all_to_all | solution.py:80
  133.8 0.0 reduce-scatter.5.cloned.1.call-start
  133.8 0.1 compare_select_fusion
  133.9 30.5 %scatter_custom_fusion.1 = s32[4096]{0:T(1024)S(1)} fusion(s32[8192]{0:T(1024)S(1)} %bitcast.62, s32[8192]{0:T(1024)S(1)} %iota.65, s32[]{:T(128)} %constant.116.clone.1), kind=kCustom, calls=%fused_computation.77 | custom fusion | bytes 16388 | tf_op jit(solution)/shard_map/scatter | solution.py:66
  164.4 2.6 copy.11
  167.0 16.3 %gather_fusion.2 = f32[4096,16]{1,0:T(8,128)} fusion(f32[8192,16]{1,0:T(8,128)} %bitcast.56, s32[4096]{0:T(1024)S(1)} %fusion.27), kind=kCustom, calls=%fused_computation.2 | custom fusion | bytes 540672 | tf_op jit(solution)/shard_map/jit(_take)/gather | solution.py:81
  183.3 2.2 copy.12
  185.4 0.7 broadcast_select_fusion
  186.2 0.0 reduce-scatter.7.cloned.1.call-start
  186.2 21.4 %reduce-scatter.5.cloned.1.call-done = f32[2,512,16]{1,2,0:T(8,128)} async-done(((f32[2,2048,16]{1,2,0:T(8,128)}), f32[2,512,16]{1,2,0:T(8,128)}) %reduce-scatter.5.cloned.1.call-update) | async-done | bytes 65552 | tf_op jit(solution)/shard_map/reduce_scatter | solution.py:83
  207.7 2.7 convolution_bitcast_fusion.1
  210.4 2.8 convolution_bitcast_fusion.2
  213.2 3.3 %copy.13 = f32[2,2,8,1536]{2,1,0,3:T(2,128)} copy(f32[2,2,8,1536]{3,2,1,0:T(8,128)S(1)} %pad_maximum_fusion) | data formatting | bytes 393216
  216.5 4.7 %reshape.276 = f32[1536,32]{1,0:T(8,128)} reshape(f32[1536,2,2,8]{3,2,1,0:T(2,128)} %bitcast.58) | data formatting | bytes 393216
  221.2 93.9 %reduce-scatter.7.cloned.1.call-done = f32[48,32]{1,0:T(8,128)} async-done(((f32[1536,32]{1,0:T(8,128)}), f32[48,32]{1,0:T(8,128)}) %reduce-scatter.7.cloned.1.call-update) | async-done | bytes 6160
  315.1 0.9 reshape.277
  315.9 0.7 copy.14
  (18 shorter events, 0.2 us)
Async XLA Ops:
  6.5 85.1 %copy-start = (bf16[8192,128]{1,0:T(8,128)(2,1)S(1)}, bf16[8192,128]{1,0:T(8,128)(2,1)}, u32[]{:S(2)}) copy-start(bf16[8192,128]{1,0:T(8,128)(2,1)} %param.4) | copy-start | bytes 6291460
  86.3 43.3 %all-to-all-start = ((s32[1,8,1024]{2,0,1:T(1,128)}), s32[1,8,1024]{2,0,1:T(1,128)S(1)}, u32[]{:S(2)}, u32[]{:S(2)}) async-start(s32[1,8,1024]{2,0,1:T(1,128)} %bitcast.4), calls=%async_computation | async-start | bytes 65536 | tf_op jit(solution)/shard_map/all_to_all | solution.py:62
  129.6 34.8 %all-to-all-start.1 = ((f32[8,1024,16]{1,2,0:T(8,128)}), f32[8,1024,16]{1,2,0:T(8,128)S(1)}, u32[]{:S(2)}, u32[]{:S(2)}) async-start(f32[8,1024,16]{1,2,0:T(8,128)} %select_select_fusion), calls=%async_computation.1 | async-start | bytes 1048576 | tf_op jit(solution)/shard_map/all_to_all | solution.py:80
  133.8 73.9 %reduce-scatter.5.cloned.1.call-start = ((), (), s32[]{:S(2)}) async-start(), calls=%async_computation.4 | async-start | bytes 327680 | tf_op jit(solution)/shard_map/reduce_scatter | solution.py:83
  186.2 128.9 %reduce-scatter.7.cloned.1.call-start = ((), (), s32[]{:S(2)}) async-start(), calls=%async_computation.5 | async-start | bytes 811008
Sparse Core Ops, SparseCore 0:
  186.3 21.3 reduce-scatter.4
  221.3 93.6 reduce-scatter.6
where the time goes:
time: 324 us; the launch traced here: 323 us
  local copies, waits for them, and re-layouts  172 us (53%)
  waiting for transfers between devices  115 us (35%)
  between operations  14.4 us (4%)
  starting transfers between devices  9.44 us (3%)
  matrix products  7.45 us (2%)
  other arithmetic  4.52 us (1%)
    unnamed x3, waiting for transfers between devices  93.9 us
    gather x1, local copies, waits for them, and re-layouts, local(): jnp.take(local_row, source_safe, axis=0)  45.5 us
    gather x2, local copies, waits for them, and re-layouts, local(): picked = jnp.take(spectra, source_safe, axis=0)  32.7 us
    scatter x1, local copies, waits for them, and re-layouts, local(): jnp.full((send_total,), -1, jnp.int32).at[send_pos]  30.5 us
    scatter x1, local copies, waits for them, and re-layouts, local(): jnp.zeros((stations * rows_les,), jnp.int32).at[arrival]  30.5 us
    reduce_scatter x1, waiting for transfers between devices, local(): lax.psum_scatter(gathered, 'modes', scatter_dimension=1, tiled=True)  21.4 us
    gather x2, local copies, waits for them, and re-layouts, local(): gathered = jnp.take(incoming, arrived_from, axis=0)  18.4 us
    unnamed x6, local copies, waits for them, and re-layouts  9.54 us
  transfers between devices with their start and end apart: 4, of which 2 were waited for; matrix products, arithmetic and copies ran while one was open for 21% of the time, Pallas kernels for 0%

commit v1 on v0

--- a/solution.py
+++ b/solution.py
@@ -6,6 +6,28 @@
 
 TIME = 512
 HARM = 8
+
+
+def cut_along(x, dim, size):
+    before, after = (x.shape[:dim], x.shape[dim + 1 :])
+    return jnp.moveaxis(x.reshape(*before, size, -1, *after), dim, 0)
+
+
+def in_order(parts, dim):
+    parts = jnp.moveaxis(parts, 0, dim)
+    shape = parts.shape
+    return parts.reshape(*shape[:dim], shape[dim] * shape[dim + 1], *shape[dim + 2 :])
+
+
+def rotated_exchange(x, axis, split_dim, concat_dim):
+    devices, index = (lax.axis_size(axis), lax.axis_index(axis))
+    tiles = cut_along(x, split_dim, devices)
+    outs = [tiles[index]]
+    for hop in range(1, devices):
+        sent = tiles[(index + hop) % devices]
+        outs.append(lax.ppermute(sent, axis, [(i, (i + hop) % devices) for i in range(devices)]))
+    tiles = jnp.stack(outs)[(index - jnp.arange(devices)) % devices]
+    return in_order(tiles, concat_dim)
 
 
 def fourier_rows():
@@ -77,7 +99,7 @@
     )
     picked = jnp.take(spectra, source_safe, axis=0)
     outgoing = jnp.where(slot_used[:, None], picked, jnp.zeros_like(picked))
-    incoming = lax.all_to_all(outgoing, "les", split_axis=0, concat_axis=0, tiled=True)
+    incoming = rotated_exchange(outgoing, "les", 0, 0)
     gathered = jnp.take(incoming, arrived_from, axis=0)
     gathered = gathered.reshape(stations, rows_les, 2 * HARM)
     summed = lax.psum_scatter(gathered, "modes", scatter_dimension=1, tiled=True)

time: 324 us -> 333 us (1.028)
  waiting for transfers between devices: 115 us -> 123 us
    ppermute x0 -> x7, waiting for transfers between devices: none -> 9.46 us  [rotated_exchange(): lax.ppermute(sent, axis, [(i, (i + hop) % devices) for i in range(devices)])]
    ppermute x0 -> x7, starting transfers between devices: none -> 5.96 us  [rotated_exchange(): lax.ppermute(sent, axis, [(i, (i + hop) % devices) for i in range(devices)])]
    all_to_all x1 -> x0, starting transfers between devices: 4.2 us -> none  [local(): lax.all_to_all(outgoing, 'les', split_axis=0, concat_axis=0, tiled=True)]
    unnamed x6 -> x12, local copies, waits for them, and re-layouts: 9.54 us -> 9.53 us
  transfers between devices with their start and end apart: 4 -> 10, of which waited for: 2 -> 4; matrix products, arithmetic and copies ran while one was open for 21% -> 20% of each run, Pallas kernels for 0% -> 0%
where the time goes in v1:
time: 333 us
  local copies, waits for them, and re-layouts  173 us (52%)
  waiting for transfers between devices  123 us (37%)
  between operations  14.6 us (4%)
  starting transfers between devices  11.2 us (3%)
  matrix products  7.45 us (2%)
  other arithmetic  3.75 us (1%)
    unnamed x3, waiting for transfers between devices  94 us
    gather x1, local copies, waits for them, and re-layouts, local(): jnp.take(local_row, source_safe, axis=0)  45.5 us
    gather x2, local copies, waits for them, and re-layouts, local(): picked = jnp.take(spectra, source_safe, axis=0)  32.7 us
    scatter x1, local copies, waits for them, and re-layouts, local(): jnp.full((send_total,), -1, jnp.int32).at[send_pos]  30.5 us
    scatter x1, local copies, waits for them, and re-layouts, local(): jnp.zeros((stations * rows_les,), jnp.int32).at[arrival]  30.5 us
    reduce_scatter x1, waiting for transfers between devices, local(): lax.psum_scatter(gathered, 'modes', scatter_dimension=1, tiled=True)  19.1 us
    gather x2, local copies, waits for them, and re-layouts, local(): gathered = jnp.take(incoming, arrived_from, axis=0)  18.4 us
    unnamed x12, local copies, waits for them, and re-layouts  9.53 us
  transfers between devices with their start and end apart: 10, of which 4 were waited for; matrix products, arithmetic and copies ran while one was open for 20% of the time, Pallas kernels for 0%

profile of v1, /device:TPU:0, one launch (start us, length us, event | category | flops | bytes accessed | tf_op | source)
XLA Modules:
  0.0 332.7 jit_solution(18415730966426722504)
XLA Ops:
  7.4 0.8 fusion.13
  8.3 0.2 reduce_window_sum.11
  8.6 0.2 fusion.5
  8.8 0.8 compare_select_fusion.2
  9.6 30.5 %scatter_custom_fusion = s32[8192]{0:T(1024)S(1)} fusion(s32[8192]{0:T(1024)S(1)} %compare_select_fusion.2, s32[8192]{0:T(1024)S(1)} %iota.68, s32[]{:T(128)} %constant.171.clone.1), kind=kCustom, calls=%fused_computation.84 | custom fusion | bytes 32772 | tf_op jit(solution)/shard_map/scatter | solution.py:78
  40.1 45.5 %gather_fusion = s32[8192]{0:T(1024)S(1)} fusion(s32[8192]{0:T(1024)S(1)} %get-tuple-element.16, s32[8192]{0:T(1024)S(1)} %maximum_clamp_fusion), kind=kCustom, calls=%fused_computation | custom fusion | bytes 98304 | tf_op jit(solution)/shard_map/jit(_take)/gather | solution.py:81
  85.6 0.6 select_select_fusion.1
  86.3 5.2 %all-to-all-start = ((s32[1,8,1024]{2,0,1:T(1,128)}), s32[1,8,1024]{2,0,1:T(1,128)S(1)}, u32[]{:S(2)}, u32[]{:S(2)}) async-start(s32[1,8,1024]{2,0,1:T(1,128)} %bitcast.4), calls=%async_computation | async-start | bytes 65536 | tf_op jit(solution)/shard_map/all_to_all | solution.py:84
  91.8 1.7 convolution_bitcast_fusion
  93.6 2.6 copy.9
  96.2 29.9 %gather_fusion.1 = f32[8192,16]{1,0:T(8,128)} fusion(f32[8192,16]{1,0:T(8,128)} %copy.9, s32[8192]{0:T(1024)S(1)} %maximum_clamp_fusion), kind=kCustom, calls=%fused_computation.1 | custom fusion | bytes 1081344 | tf_op jit(solution)/shard_map/jit(_take)/gather | solution.py:100
  126.1 2.8 copy.10
  129.1 2.6 collective-permute-start.6
  131.7 0.6 collective-permute-start.5
  132.3 1.4 collective-permute-start.3
  133.8 1.2 collective-permute-start
  135.1 30.5 %scatter_custom_fusion.1 = s32[4096]{0:T(1024)S(1)} fusion(s32[8192]{0:T(1024)S(1)} %bitcast.92, s32[8192]{0:T(1024)S(1)} %iota.69, s32[]{:T(128)} %constant.170.clone.1), kind=kCustom, calls=%fused_computation.93 | custom fusion | bytes 16388 | tf_op jit(solution)/shard_map/scatter | solution.py:88
  165.7 5.1 %collective-permute-done.1 = f32[1024,16]{0,1:T(8,128)S(1)} collective-permute-done((f32[1024,16]{0,1:T(8,128)S(1)}, f32[1024,16]{0,1:T(8,128)S(1)}, u32[]{:S(2)}, u32[]{:S(2)}) %collective-permute-start.1) | collective-permute-done | bytes 65568 | tf_op jit(solution)/shard_map/ppermute | solution.py:28
  170.8 4.3 %collective-permute-done.2 = f32[1024,16]{0,1:T(8,128)S(1)} collective-permute-done((f32[1024,16]{0,1:T(8,128)S(1)}, f32[1024,16]{0,1:T(8,128)S(1)}, u32[]{:S(2)}, u32[]{:S(2)}) %collective-permute-start.2) | collective-permute-done | bytes 65568 | tf_op jit(solution)/shard_map/ppermute | solution.py:28
  175.3 0.6 gather_fusion.2
  175.8 2.6 copy.11
  178.5 16.3 %gather_fusion.3 = f32[4096,16]{1,0:T(8,128)} fusion(f32[8192,16]{1,0:T(8,128)} %bitcast.86, s32[4096]{0:T(1024)S(1)} %fusion.27), kind=kCustom, calls=%fused_computation.3 | custom fusion | bytes 540672 | tf_op jit(solution)/shard_map/jit(_take)/gather | solution.py:103
  194.7 2.2 copy.12
  196.9 0.7 broadcast_select_fusion
  197.7 19.1 %reduce-scatter.5.cloned.1.call-done = f32[2,512,16]{1,2,0:T(8,128)} async-done(((f32[2,2048,16]{1,2,0:T(8,128)}), f32[2,512,16]{1,2,0:T(8,128)}) %reduce-scatter.5.cloned.1.call-update) | async-done | bytes 65552 | tf_op jit(solution)/shard_map/reduce_scatter | solution.py:105
  216.8 2.7 convolution_bitcast_fusion.1
  219.6 2.8 convolution_bitcast_fusion.2
  222.4 3.3 copy.13
  225.6 4.7 %reshape.336 = f32[1536,32]{1,0:T(8,128)} reshape(f32[1536,2,2,8]{3,2,1,0:T(2,128)} %bitcast.88) | data formatting | bytes 393216
  230.3 94.0 %reduce-scatter.7.cloned.1.call-done = f32[48,32]{1,0:T(8,128)} async-done(((f32[1536,32]{1,0:T(8,128)}), f32[48,32]{1,0:T(8,128)}) %reduce-scatter.7.cloned.1.call-update) | async-done | bytes 6160
  324.3 0.9 reshape.337
  325.2 0.7 copy.14
  (41 shorter events, 1.0 us)
Async XLA Ops:
  6.5 85.3 %copy-start = (bf16[8192,128]{1,0:T(8,128)(2,1)S(1)}, bf16[8192,128]{1,0:T(8,128)(2,1)}, u32[]{:S(2)}) copy-start(bf16[8192,128]{1,0:T(8,128)(2,1)} %param.4) | copy-start | bytes 6291460
  86.3 48.7 %all-to-all-start = ((s32[1,8,1024]{2,0,1:T(1,128)}), s32[1,8,1024]{2,0,1:T(1,128)S(1)}, u32[]{:S(2)}, u32[]{:S(2)}) async-start(s32[1,8,1024]{2,0,1:T(1,128)} %bitcast.4), calls=%async_computation | async-start | bytes 65536 | tf_op jit(solution)/shard_map/all_to_all | solution.py:84
  91.4 125.4 %reduce-scatter.5.cloned.1.call-start = ((), (), s32[]{:S(2)}) async-start(), calls=%async_computation.3 | async-start | bytes 327680 | tf_op jit(solution)/shard_map/reduce_scatter | solution.py:105
  129.1 46.2 %collective-permute-start.6 = (f32[1024,16]{0,1:T(8,128)S(1)}, f32[1024,16]{0,1:T(8,128)S(1)}, u32[]{:S(2)}, u32[]{:S(2)}) collective-permute-start(f32[1024,16]{0,1:T(8,128)S(1)} %get-tuple-element.8), channel_id=1, source_target_pairs={{0,28},{4,0},{8,4},{12,8},{16,12},{20,16},{24,20},{28,24},{1,29},{... | collective-permute-start | bytes 196616 | tf_op jit(solution)/shard_map/ppermute | solution.py:28
  131.7 43.6 %collective-permute-start.5 = (f32[1024,16]{0,1:T(8,128)S(1)}, f32[1024,16]{0,1:T(8,128)S(1)}, u32[]{:S(2)}, u32[]{:S(2)}) collective-permute-start(f32[1024,16]{0,1:T(8,128)S(1)} %get-tuple-element.9), channel_id=1, source_target_pairs={{0,24},{4,28},{8,0},{12,4},{16,8},{20,12},{24,16},{28,20},{1,25},{... | collective-permute-start | bytes 196616 | tf_op jit(solution)/shard_map/ppermute | solution.py:28
  132.2 43.0 %collective-permute-start.4 = (f32[1024,16]{0,1:T(8,128)S(1)}, f32[1024,16]{0,1:T(8,128)S(1)}, u32[]{:S(2)}, u32[]{:S(2)}) collective-permute-start(f32[1024,16]{0,1:T(8,128)S(1)} %get-tuple-element.10), channel_id=1, source_target_pairs={{0,20},{4,24},{8,28},{12,0},{16,4},{20,8},{24,12},{28,16},{1,21},{... | collective-permute-start | bytes 196616 | tf_op jit(solution)/shard_map/ppermute | solution.py:28
  132.3 42.8 %collective-permute-start.3 = (f32[1024,16]{0,1:T(8,128)S(1)}, f32[1024,16]{0,1:T(8,128)S(1)}, u32[]{:S(2)}, u32[]{:S(2)}) collective-permute-start(f32[1024,16]{0,1:T(8,128)S(1)} %get-tuple-element.11), channel_id=1, source_target_pairs={{0,16},{4,20},{8,24},{12,28},{16,0},{20,4},{24,8},{28,12},{1,17},{... | collective-permute-start | bytes 196616 | tf_op jit(solution)/shard_map/ppermute | solution.py:28
  133.8 31.8 %collective-permute-start = (f32[1024,16]{0,1:T(8,128)S(1)}, f32[1024,16]{0,1:T(8,128)S(1)}, u32[]{:S(2)}, u32[]{:S(2)}) collective-permute-start(f32[1024,16]{0,1:T(8,128)S(1)} %get-tuple-element.14), channel_id=1, source_target_pairs={{0,4},{4,8},{8,12},{12,16},{16,20},{20,24},{24,28},{28,0},{1,5},{5... | collective-permute-start | bytes 196616 | tf_op jit(solution)/shard_map/ppermute | solution.py:28
  165.6 5.2 %collective-permute-start.1 = (f32[1024,16]{0,1:T(8,128)S(1)}, f32[1024,16]{0,1:T(8,128)S(1)}, u32[]{:S(2)}, u32[]{:S(2)}) collective-permute-start(f32[1024,16]{0,1:T(8,128)S(1)} %get-tuple-element.13), channel_id=1, source_target_pairs={{0,8},{4,12},{8,16},{12,20},{16,24},{20,28},{24,0},{28,4},{1,9},{5... | collective-permute-start | bytes 196616 | tf_op jit(solution)/shard_map/ppermute | solution.py:28
  170.8 4.3 %collective-permute-start.2 = (f32[1024,16]{0,1:T(8,128)S(1)}, f32[1024,16]{0,1:T(8,128)S(1)}, u32[]{:S(2)}, u32[]{:S(2)}) collective-permute-start(f32[1024,16]{0,1:T(8,128)S(1)} %get-tuple-element.12), channel_id=1, source_target_pairs={{0,12},{4,16},{8,20},{12,24},{16,28},{20,0},{24,4},{28,8},{1,13},{... | collective-permute-start | bytes 196616 | tf_op jit(solution)/shard_map/ppermute | solution.py:28
  197.7 126.6 %reduce-scatter.7.cloned.1.call-start = ((), (), s32[]{:S(2)}) async-start(), calls=%async_computation.4 | async-start | bytes 811008
Sparse Core Ops, SparseCore 0:
  197.8 19.0 reduce-scatter.4
  230.4 93.7 reduce-scatter.6
